TPU v7x, 32 devices: a whole 2x2x4 slice. The times are simulated.
32 devices in a mesh: groups: 2 (over y), seq: 4 (over z), head: 2 (over x), batch: 2 (over core).
Axes of the slice: x: 2, y: 2, z: 4, core: 2. Of those that a mesh axis runs over, the one named last changes fastest.
Arguments:
- queries: bfloat16 [4, 512, 2560], P(('groups', 'batch'), 'seq', 'head'), parts along dimension 0, may hold values from -6 to 6
- keys: bfloat16 [4, 512, 2560], P(('groups', 'batch'), 'seq', 'head'), parts along dimension 0, may hold values from -6 to 6
- values: bfloat16 [4, 512, 2560], P(('groups', 'batch'), 'seq', 'head'), parts along dimension 0, may hold values from -6 to 6
- cache_keys: bfloat16 [4, 8, 32, 2560], P(('groups', 'batch'), 'seq', None, 'head'), parts along dimension 0, may hold values from -6 to 6
- cache_values: bfloat16 [4, 8, 32, 2560], P(('groups', 'batch'), 'seq', None, 'head'), parts along dimension 0, may hold values from -6 to 6
- frame_list: int32 [4, 3], P(('groups', 'batch')), parts along dimension 0, may hold values from 0 to 7, as said below
- frame_place: int32 [4, 8], P(('groups', 'batch')), parts along dimension 0, may hold values from 0 to 7, each once within a row
- tile_mask: int32 [4, 4, 4], P(('groups', 'batch'), 'seq'), parts along dimension 0, may hold values from 0 to 1, as said below
Outputs:
- attention: bfloat16 [4, 512, 2560], P(('groups', 'batch'), 'seq', 'head'), parts along dimension 0
There are 2 independent parts, one for each index of `groups`. A program takes and returns all parts, laid end to end along the dimension named above; each array names one. Nothing has to cross between parts.
Inputs may be any that keep to these rules, and one draw needn't show every extreme that they name: `frame_list`: each row holds frame 0 and then 3 - 1 consecutive frame numbers. `tile_mask`: ones on the diagonal of each video's tile matrix.
All inputs are finite; a program needn't handle non-finite values.
Results may differ from a plain program's by a relative error of at most 0.006.
Values may be sent and summed in bfloat16 or wider, within the bound.
No kernel may reach another device: no remote copies, remote signals or barrier semaphores. Data moves between devices by JAX's collectives and lax.ppermute only.
A program may use at most 128 MiB of HBM per device.

v0:
```python
import math
import jax
import jax.numpy as jnp
from jax import lax
from jax.sharding import PartitionSpec as P

HD = 128
TILE = 128
NEG_FILL = -1e30


def attend(running, key_part, value_part, live, query_heads):
    videos, length, col_count = key_part.shape
    head_count = col_count // HD

    def update(previous):
        peak_old, total_old, summed_old = previous
        key_heads = key_part.reshape(videos, length, head_count, HD)
        value_heads = value_part.reshape(videos, length, head_count, HD)
        scores = jnp.einsum(
            "vqhd,vkhd->vhqk", query_heads, key_heads, preferred_element_type=jnp.float32
        ) * (1.0 / math.sqrt(HD))
        allowed = live[:, None, :, :]
        scores = jnp.where(allowed, scores, NEG_FILL)
        peak_new = jnp.maximum(peak_old, jnp.max(scores, axis=3))
        weights = jnp.where(allowed, jnp.exp(scores - peak_new[..., None]), 0.0)
        factor = jnp.exp(peak_old - peak_new)
        total_new = total_old * factor + jnp.sum(weights, axis=3)
        product = jnp.einsum(
            "vhqk,vkhd->vhqd",
            weights.astype(jnp.bfloat16),
            value_heads,
            preferred_element_type=jnp.float32,
        )
        summed_new = summed_old * factor[..., None] + product
        return (peak_new, total_new, summed_new)

    def unchanged(previous):
        return previous

    return lax.cond(jnp.any(live), update, unchanged, running)


def body(queries, keys, values, cache_keys, cache_values, frame_list, frame_place, tile_mask):
    videos, tok_rows, col_count = queries.shape
    head_count = col_count // HD
    query_heads = queries.reshape(videos, tok_rows, head_count, HD)
    running = (
        jnp.full((videos, head_count, tok_rows), NEG_FILL, jnp.float32),
        jnp.zeros((videos, head_count, tok_rows), jnp.float32),
        jnp.zeros((videos, head_count, tok_rows, HD), jnp.float32),
    )
    frame_tok = cache_keys.shape[2]
    listed = jnp.any(frame_place[:, :, None] == frame_list[:, None, :], axis=2)
    key_piece = lax.all_gather(cache_keys, "seq", axis=1, tiled=True)
    value_piece = lax.all_gather(cache_values, "seq", axis=1, tiled=True)
    count_frames = key_piece.shape[1]
    token_flags = jnp.repeat(listed, frame_tok, axis=1)
    live = jnp.broadcast_to(token_flags[:, None, :], (videos, tok_rows, count_frames * frame_tok))
    key_flat = key_piece.reshape(videos, count_frames * frame_tok, col_count)
    value_flat = value_piece.reshape(videos, count_frames * frame_tok, col_count)
    running = attend(running, key_flat, value_flat, live, query_heads)
    key_piece = lax.all_gather(keys, "seq", axis=1, tiled=True)
    value_piece = lax.all_gather(values, "seq", axis=1, tiled=True)
    length = key_piece.shape[1]
    key_tiles = jnp.arange(length, dtype=jnp.int32) // TILE
    tile_live = jnp.take(tile_mask, key_tiles, axis=2)
    running = attend(
        running, key_piece, value_piece, jnp.repeat(tile_live, TILE, axis=1) > 0, query_heads
    )
    peak, total, summed = running
    result = summed / total[..., None]
    return result.transpose(0, 2, 1, 3).reshape(videos, tok_rows, col_count).astype(jnp.bfloat16)


def solution(mesh):
    return jax.shard_map(
        body,
        mesh=mesh,
        in_specs=(
            P(("groups", "batch"), "seq", "head"),
            P(("groups", "batch"), "seq", "head"),
            P(("groups", "batch"), "seq", "head"),
            P(("groups", "batch"), "seq", None, "head"),
            P(("groups", "batch"), "seq", None, "head"),
            P(("groups", "batch"), None),
            P(("groups", "batch"), None),
            P(("groups", "batch"), "seq", None),
        ),
        out_specs=P(("groups", "batch"), "seq", "head"),
        check_vma=False,
    )
```

profile of v0, /device:TPU:0, one launch (start us, length us, event | category | flops | bytes accessed | tf_op | source)
XLA Modules:
  0.0 110.2 jit_solution(18014833076720647111)
XLA Ops:
  6.5 0.0 copy-start.3
  6.5 0.0 copy-start.5
  6.5 0.0 copy-start.6
  6.5 0.0 copy-start
  6.5 0.0 copy-start.1
  6.5 0.0 all-gather.3.cloned.1.call-start
  6.6 1.9 %copy.50 = bf16[1,128,1280]{1,2,0:T(8,128)(2,1)} copy(bf16[1,128,1280]{2,1,0:T(8,128)(2,1)} %param.13) | data formatting | bytes 655360 | tf_op args[1]
  8.5 0.0 all-gather.3.cloned.1.call-update
  8.6 0.0 copy-start.2
  8.6 0.0 all-gather.5.cloned.1.call-start
  8.6 1.9 %copy.51 = bf16[1,128,1280]{1,2,0:T(8,128)(2,1)} copy(bf16[1,128,1280]{2,1,0:T(8,128)(2,1)} %param.14) | data formatting | bytes 655360 | tf_op args[2]
  10.5 0.0 all-gather.5.cloned.1.call-update
  10.5 0.0 copy-done.3
  10.6 0.7 fusion.41
  11.2 2.7 %compare_select_fusion.1 = s32[512,1]{0,1:T(1,128)S(1)} fusion(s32[]{:T(128)} %bitcast.15, s32[]{:T(128)} %bitcast.16, s32[]{:T(128)} %bitcast.18, s32[]{:T(128)} %bitcast.17), kind=kLoop, calls=%fused_computation.45 | loop fusion | flops 8704 | bytes 2064 | tf_op jit(solution)/shard_map/jit(_take)/gather | solution.py:67
  14.0 0.8 broadcast_reduce_fusion
  15.4 0.0 copy-done.5
  15.4 0.0 copy-done.6
  15.4 0.1 compare_reduce_fusion
  15.5 0.1 broadcast_in_dim.88
  15.6 0.1 broadcast_in_dim.89
  15.7 0.7 broadcast_reduce_fusion.1
  17.1 0.0 copy-done
  17.2 0.2 copy.44
  17.4 0.0 copy-done.1
  17.4 27.2 %all_gather.12 = bf16[1,8,32,1280]{3,2,0,1:T(8,128)(2,1)S(1)} all-gather(bf16[1,2,32,1280]{3,2,0,1:T(8,128)(2,1)S(1)} %bitcast.73), channel_id=1, replica_groups=mesh['groups'=2,'seq'=4,'head'=2,'batch'=2] {'seq'}, dimensions={1}, use_global_device_ids=true | all-gather | bytes 819200 | tf_op jit(solution)/shard_map/all_gather | solution.py:55
  44.6 0.0 copy-done.2
  44.6 21.8 %all_gather.13 = bf16[1,8,32,1280]{3,2,0,1:T(8,128)(2,1)S(1)} all-gather(bf16[1,2,32,1280]{3,2,0,1:T(8,128)(2,1)S(1)} %bitcast.74), channel_id=1, replica_groups=mesh['groups'=2,'seq'=4,'head'=2,'batch'=2] {'seq'}, dimensions={1}, use_global_device_ids=true | all-gather | bytes 819200 | tf_op jit(solution)/shard_map/all_gather | solution.py:56
  66.3 3.3 %conditional.2 = (f32[1,10,128]{2,1,0:T(8,128)S(1)}, f32[1,10,128]{2,1,0:T(8,128)S(1)}, f32[1,10,128,128]{3,2,1,0:T(8,128)}) conditional(s32[]{:T(128)} %convert_element_type.32, () %tuple.20, (pred[8]{0:T(512)(128)(4,1)S(1)}, bf16[1,128,10,128]{1,3,2,0:T(8,128)(2,1)S(1)}, bf16[1,8,32,1280]{3,2,0,1:T(8,128)(2,1)S(1)}, ...), branch_computations={%region_3.4_spmd, %region_4.7_spmd} | conditional | flops 170891520 | bytes 8910368 | solution.py:41
  66.3 0.4 reshape.260
  66.7 0.1 broadcast_in_dim.71
  66.8 0.1 reshape.258
  66.9 0.5 fusion.40
  67.4 0.5 fusion.3
  67.9 0.4 reshape.261
  68.3 1.3 %fusion.1 = f32[1,10,128,128]{3,2,1,0:T(8,128)} fusion(f32[10,128,256]{2,1,0:T(8,128)S(1)} %get-tuple-element.99, bf16[256,10,128]{2,1,0:T(8,128)(2,1)S(1)} %reshape.261, f32[10,128]{1,0:T(8,128)S(1)} %get-tuple-element.97, pred[256]{0:T(512)(128)(4,1)S(1)} %reshape.258, f32[10,128]{1,0:T(8,128)S(1)} %get-tuple-element.96), kind=kOutput, calls=%fused_computation.4 | convolution fusion | flops 85032960 | bytes 2631936 | tf_op jit(solution)/shard_map/cond/branch_1_fun/vhqk,vkhd->vhqd/dot_general | solution.py:29
  69.6 0.0 all-gather.3.cloned.1.call-done
  69.6 26.9 %all-gather.5.cloned.1.call-done = bf16[1,512,1280]{1,2,0:T(8,128)(2,1)} async-done(((bf16[1,128,1280]{1,2,0:T(8,128)(2,1)}), bf16[1,512,1280]{1,2,0:T(8,128)(2,1)}) %all-gather.5.cloned.1.call-update) | async-done | bytes 1310736 | tf_op jit(solution)/shard_map/all_gather | solution.py:64
  96.6 5.8 %conditional.3 = (f32[1,10,128]{2,1,0:T(8,128)S(1)}, f32[1,10,128,128]{2,3,1,0:T(8,128)S(1)}) conditional(s32[]{:T(128)} %convert_element_type.31, (f32[1,10,128]{2,1,0:T(8,128)S(1)}, f32[1,10,128,128]{3,2,1,0:T(8,128)}) %tuple.22, (pred[1,128,512]{2,1,0:T(8,128)(4,1)S(1)}, bf16[1,128,10,128]{1,3,2,0:T(8,128)(2,1)S(1)}, ...), branch_computations={%region_7.8_spmd, %region_8.11_spmd} | conditional | flops 344396800 | bytes 18946092 | solution.py:41
  96.6 2.0 %fusion.13 = (f32[10,128]{1,0:T(8,128)S(1)}, f32[10,128,512]{2,1,0:T(8,128)S(1)}) fusion(pred[128,512]{1,0:T(8,128)(4,1)S(1)} %bitcast.70, bf16[512,10,128]{0,2,1:T(8,128)(2,1)} %bitcast.68, bf16[1,128,10,128]{1,3,2,0:T(8,128)(2,1)S(1)} %get-tuple-element.81), kind=kOutput, calls=%fused_computation.20 | convolution fusion | flops 169736960 | bytes 4330496 | tf_op jit(solution)/shard_map/cond/branch_1_fun/vqhd,vkhd->vhqk/dot_general | solution.py:20
  98.6 0.0 copy-start.4
  98.7 0.9 fusion.15
  99.5 0.4 copy-done.4
  100.0 2.2 %fusion.26 = f32[1,10,128,128]{3,2,1,0:T(8,128)S(1)} fusion(bf16[512,10,128]{0,2,1:T(8,128)(2,1)S(1)} %bitcast.77, f32[10,128,512]{2,1,0:T(8,128)S(1)} %get-tuple-element.95, f32[10,128]{1,0:T(8,128)S(1)} %get-tuple-element.93, pred[128,512]{1,0:T(8,128)(4,1)S(1)} %bitcast.72, f32[1,10,128,128]{3,2,1,0:T(8,128)} %get-tuple-element.42, ...), kind=kOutput, calls=%fused_computation.30 | convolution fusion | flops 171376640 | bytes 5318656 | tf_op jit(solution)/shard_map/cond/branch_1_fun/vhqk,vkhd->vhqd/dot_general | solution.py:29
  102.1 0.2 copy.58
  102.4 0.1 divide_convert_fusion
  102.4 0.9 copy.54
  (6 shorter events, 0.1 us)
Async XLA Ops:
  6.5 4.0 %copy-start.3 = (s32[1,1,4]{2,1,0:T(1,128)S(1)}, s32[1,1,4]{2,1,0:T(1,128)}, u32[]{:S(2)}) copy-start(s32[1,1,4]{2,1,0:T(1,128)} %param.19) | copy-start | bytes 52
  6.5 8.9 %copy-start.5 = (s32[1,8]{1,0:T(1,128)S(1)}, s32[1,8]{1,0:T(1,128)}, u32[]{:S(2)}) copy-start(s32[1,8]{1,0:T(1,128)} %param.18) | copy-start | bytes 100
  6.5 8.9 %copy-start.6 = (s32[1,3]{1,0:T(1,128)S(1)}, s32[1,3]{1,0:T(1,128)}, u32[]{:S(2)}) copy-start(s32[1,3]{1,0:T(1,128)} %param.17) | copy-start | bytes 40
  6.5 10.6 %copy-start = (bf16[1,128,1280]{2,1,0:T(8,128)(2,1)S(1)}, bf16[1,128,1280]{2,1,0:T(8,128)(2,1)}, u32[]{:S(2)}) copy-start(bf16[1,128,1280]{2,1,0:T(8,128)(2,1)} %param.12) | copy-start | bytes 983044
  6.5 10.8 %copy-start.1 = (bf16[1,2,32,1280]{3,2,1,0:T(8,128)(2,1)S(1)}, bf16[1,2,32,1280]{3,2,1,0:T(8,128)(2,1)}, u32[]{:S(2)}) copy-start(bf16[1,2,32,1280]{3,2,1,0:T(8,128)(2,1)} %param.15) | copy-start | bytes 491524
  6.5 63.1 %all-gather.3.cloned.1.call-start = ((), (), s32[]{:S(2)}) async-start(), calls=%async_computation | async-start | bytes 1638400 | tf_op jit(solution)/shard_map/all_gather | solution.py:63
  8.6 36.0 %copy-start.2 = (bf16[1,2,32,1280]{3,2,1,0:T(8,128)(2,1)S(1)}, bf16[1,2,32,1280]{3,2,1,0:T(8,128)(2,1)}, u32[]{:S(2)}) copy-start(bf16[1,2,32,1280]{3,2,1,0:T(8,128)(2,1)} %param.16) | copy-start | bytes 491524
  8.6 88.0 %all-gather.5.cloned.1.call-start = ((), (), s32[]{:S(2)}) async-start(), calls=%async_computation.1 | async-start | bytes 1638400 | tf_op jit(solution)/shard_map/all_gather | solution.py:64
  98.6 1.3 %copy-start.4 = (bf16[1,512,1280]{1,2,0:T(8,128)(2,1)S(1)}, bf16[1,512,1280]{1,2,0:T(8,128)(2,1)}, u32[]{:S(2)}) copy-start(bf16[1,512,1280]{1,2,0:T(8,128)(2,1)} %get-tuple-element.43) | copy-start | bytes 3932164 | tf_op jit(solution)/shard_map/cond
Sparse Core Ops, SparseCore 0:
  8.9 54.7 all-gather.2
  65.3 31.2 all-gather.4
where the time goes:
time: 111 us; the launch traced here: 110 us
  blocking collectives  49 us (44%)
  waiting for transfers between devices  27 us (24%)
  between operations  14.9 us (13%)
  local copies, waits for them, and re-layouts  7.46 us (7%)
  matrix products  5.99 us (5%)
  other arithmetic  5.75 us (5%)
    all_gather x1, blocking collectives, body(): key_piece = lax.all_gather(cache_keys, 'seq', axis=1, tiled=True)  27.2 us
    all_gather x1, waiting for transfers between devices, body(): value_piece = lax.all_gather(values, 'seq', axis=1, tiled=True)  26.9 us
    all_gather x1, blocking collectives, body(): value_piece = lax.all_gather(cache_values, 'seq', axis=1, tiled=True)  21.8 us
    unnamed x15, local copies, waits for them, and re-layouts  4.08 us
    dot_general x2, matrix products, update(): jnp.einsum('vhqk,vkhd->vhqd', weights.astype(jnp.bfloat16), value_heads,...  3.49 us
    gather x1, other arithmetic, body(): tile_live = jnp.take(tile_mask, key_tiles, axis=2)  2.7 us
    dot_general x2, matrix products, update(): jnp.einsum('vqhd,vkhd->vhqk', query_heads, key_heads, preferred_element_t...  2.5 us
  transfers between devices with their start and end apart: 2, of which 1 were waited for; matrix products, arithmetic and copies ran while one was open for 10% of the time, Pallas kernels for 0%

commit v1 on v0

--- a/solution.py
+++ b/solution.py
@@ -52,7 +52,12 @@
     )
     frame_tok = cache_keys.shape[2]
     listed = jnp.any(frame_place[:, :, None] == frame_list[:, None, :], axis=2)
-    key_piece = lax.all_gather(cache_keys, "seq", axis=1, tiled=True)
+    ring = [cache_keys]
+    for hop in range(3):
+        ring.append(lax.ppermute(ring[-1], "seq", [(dev, (dev + 1) % 4) for dev in range(4)]))
+    key_piece = jnp.roll(
+        jnp.concatenate(ring[::-1], axis=1), (lax.axis_index("seq") + 1) * ring[0].shape[1], axis=1
+    )
     value_piece = lax.all_gather(cache_values, "seq", axis=1, tiled=True)
     count_frames = key_piece.shape[1]
     token_flags = jnp.repeat(listed, frame_tok, axis=1)

time: 111 us -> 107 us (0.964)
  blocking collectives: 49 us -> 22.7 us
  waiting for transfers between devices: 27 us -> 46.5 us
  starting transfers between devices: 0.08 us -> 3.22 us
    all_gather x1 -> x0, blocking collectives: 27.2 us -> none  [body(): key_piece = lax.all_gather(cache_keys, 'seq', axis=1, tiled=True)]
    ppermute x0 -> x3, waiting for transfers between devices: none -> 14.8 us  [body(): lax.ppermute(ring[-1], 'seq', [(dev, (dev + 1) % 4) for dev in range(4)])]
    all_gather x1, waiting for transfers between devices: 26.9 us -> 31.7 us  [body(): value_piece = lax.all_gather(values, 'seq', axis=1, tiled=True)]
    ppermute x0 -> x3, starting transfers between devices: none -> 3.14 us  [body(): lax.ppermute(ring[-1], 'seq', [(dev, (dev + 1) % 4) for dev in range(4)])]
    unnamed x15 -> x22, local copies, waits for them, and re-layouts: 4.08 us -> 4.17 us
  transfers between devices with their start and end apart: 2 -> 5, of which waited for: 1 -> 3; matrix products, arithmetic and copies ran while one was open for 10% -> 10% of each run, Pallas kernels for 0% -> 0%
where the time goes in v1:
time: 107 us
  waiting for transfers between devices  46.5 us (43%)
  blocking collectives  22.7 us (21%)
  between operations  15 us (14%)
  local copies, waits for them, and re-layouts  7.54 us (7%)
  matrix products  6.03 us (6%)
  other arithmetic  5.46 us (5%)
  starting transfers between devices  3.22 us (3%)
    all_gather x1, waiting for transfers between devices, body(): value_piece = lax.all_gather(values, 'seq', axis=1, tiled=True)  31.7 us
    all_gather x1, blocking collectives, body(): value_piece = lax.all_gather(cache_values, 'seq', axis=1, tiled=True)  22.7 us
    ppermute x3, waiting for transfers between devices, body(): lax.ppermute(ring[-1], 'seq', [(dev, (dev + 1) % 4) for dev in range(4)])  14.8 us
    unnamed x22, local copies, waits for them, and re-layouts  4.17 us
    dot_general x2, matrix products, update(): jnp.einsum('vhqk,vkhd->vhqd', weights.astype(jnp.bfloat16), value_heads,...  3.65 us
    ppermute x3, starting transfers between devices, body(): lax.ppermute(ring[-1], 'seq', [(dev, (dev + 1) % 4) for dev in range(4)])  3.14 us
    gather x1, other arithmetic, body(): tile_live = jnp.take(tile_mask, key_tiles, axis=2)  2.62 us
    dot_general x2, matrix products, update(): jnp.einsum('vqhd,vkhd->vhqk', query_heads, key_heads, preferred_element_t...  2.38 us
  transfers between devices with their start and end apart: 5, of which 3 were waited for; matrix products, arithmetic and copies ran while one was open for 10% of the time, Pallas kernels for 0%

profile of v1, /device:TPU:0, one launch (start us, length us, event | category | flops | bytes accessed | tf_op | source)
XLA Modules:
  0.0 106.6 jit_solution(9822175464285835835)
XLA Ops:
  6.5 0.0 copy-start.2
  6.5 0.0 copy-start.3
  6.5 0.0 copy-start.5
  6.5 0.0 copy-start.6
  6.5 0.0 copy-start.1
  6.5 0.0 all-gather.3.cloned.1.call-start
  6.6 2.0 %copy.49 = bf16[1,128,1280]{1,2,0:T(8,128)(2,1)} copy(bf16[1,128,1280]{2,1,0:T(8,128)(2,1)} %param.13) | data formatting | bytes 655360 | tf_op args[1]
  8.6 0.0 all-gather.3.cloned.1.call-update
  8.6 0.0 all-gather.5.cloned.1.call-start
  8.6 3.1 %collective-permute-start = (bf16[1,2,32,1280]{3,2,1,0:T(8,128)(2,1)}, bf16[1,2,32,1280]{3,2,1,0:T(8,128)(2,1)S(1)}, u32[]{:S(2)}, u32[]{:S(2)}) collective-permute-start(bf16[1,2,32,1280]{3,2,1,0:T(8,128)(2,1)} %param.15), channel_id=1, source_target_pairs={{0,4},{4,8},{8,12},{12,0},{1,5},{5,9},{9,13},{13,1},{2,6},{6,10},{... | collective-permute-start | bytes 491528 | tf_op jit(solution)/shard_map/ppermute | solution.py:57
  11.7 1.9 %copy.50 = bf16[1,128,1280]{1,2,0:T(8,128)(2,1)} copy(bf16[1,128,1280]{2,1,0:T(8,128)(2,1)} %param.14) | data formatting | bytes 655360 | tf_op args[2]
  13.6 0.0 all-gather.5.cloned.1.call-update
  13.6 0.0 copy-start
  13.6 0.0 copy-done.2
  13.6 22.7 %all_gather.9 = bf16[1,8,32,1280]{3,2,0,1:T(8,128)(2,1)S(1)} all-gather(bf16[1,2,32,1280]{3,2,0,1:T(8,128)(2,1)S(1)} %bitcast.72), channel_id=1, replica_groups=mesh['groups'=2,'seq'=4,'head'=2,'batch'=2] {'seq'}, dimensions={1}, use_global_device_ids=true | all-gather | bytes 819200 | tf_op jit(solution)/shard_map/all_gather | solution.py:61
  36.4 0.0 copy-done.3
  36.4 0.7 fusion.42
  37.1 2.6 %compare_select_fusion.1 = s32[512,1]{0,1:T(1,128)S(1)} fusion(s32[]{:T(128)} %bitcast.15, s32[]{:T(128)} %bitcast.16, s32[]{:T(128)} %bitcast.18, s32[]{:T(128)} %bitcast.17), kind=kLoop, calls=%fused_computation.55 | loop fusion | flops 8704 | bytes 2064 | tf_op jit(solution)/shard_map/jit(_take)/gather | solution.py:72
  39.7 0.0 collective-permute-done
  39.7 0.1 collective-permute-start.1
  39.8 0.0 copy-done.5
  39.8 0.0 copy-done.6
  39.8 0.1 compare_reduce_fusion
  39.9 10.6 %collective-permute-done.1 = bf16[1,2,32,1280]{3,2,1,0:T(8,128)(2,1)S(1)} collective-permute-done((bf16[1,2,32,1280]{3,2,1,0:T(8,128)(2,1)S(1)}, bf16[1,2,32,1280]{3,2,1,0:T(8,128)(2,1)S(1)}, u32[]{:S(2)}, u32[]{:S(2)}) %collective-permute-start.1) | collective-permute-done | bytes 163872 | tf_op jit(solution)/shard_map/ppermute | solution.py:57
  50.5 0.0 collective-permute-start.2
  50.5 0.8 broadcast_reduce_fusion
  52.0 0.1 broadcast_in_dim.88
  52.1 0.1 broadcast_in_dim.89
  52.1 0.7 broadcast_reduce_fusion.1
  53.6 0.0 copy-done.1
  53.6 0.2 copy.45
  53.8 4.2 %collective-permute-done.2 = bf16[1,2,32,1280]{3,2,1,0:T(8,128)(2,1)S(1)} collective-permute-done((bf16[1,2,32,1280]{3,2,1,0:T(8,128)(2,1)S(1)}, bf16[1,2,32,1280]{3,2,1,0:T(8,128)(2,1)S(1)}, u32[]{:S(2)}, u32[]{:S(2)}) %collective-permute-start.2) | collective-permute-done | bytes 163872 | tf_op jit(solution)/shard_map/ppermute | solution.py:57
  58.1 0.0 copy-done
  58.2 3.1 %conditional.2 = (f32[1,10,128]{2,1,0:T(8,128)S(1)}, f32[1,10,128]{2,1,0:T(8,128)S(1)}, f32[1,10,128,128]{3,2,1,0:T(8,128)}) conditional(s32[]{:T(128)} %convert_element_type.35, () %tuple.31, (pred[8,32]{1,0:T(8,128)(4,1)S(1)}, s32[]{:T(128)}, s32[]{:T(128)}, bf16[1,16,32,1280]{3,2,1,0:T(8,128)(2,1)S(1)}, bf16[1,128,10,128]{1,3,2,0:T(8,128)(2,1)S(1)}, ...), branch_computations={%region_3.4_spmd, %region_4.7_spmd} | conditional | flops 170891536 | bytes 10220983 | solution.py:41
  58.2 0.1 constant_dynamic-slice_fusion
  58.3 0.4 reshape.285
  58.7 0.1 reshape.284
  58.8 0.4 fusion.41
  59.1 0.3 fusion.4
  59.4 0.4 reshape.287
  59.8 1.5 %fusion.2 = f32[1,10,128,128]{3,2,1,0:T(8,128)} fusion(f32[10,128,256]{1,2,0:T(8,128)S(1)} %get-tuple-element.208, bf16[256,10,128]{2,1,0:T(8,128)(2,1)S(1)} %reshape.287, f32[10,128]{1,0:T(8,128)S(1)} %get-tuple-element.206, pred[256]{0:T(512)(128)(4,1)S(1)} %reshape.284, f32[10,128]{1,0:T(8,128)S(1)} %get-tuple-element.205), kind=kOutput, calls=%fused_computation.5 | convolution fusion | flops 85032960 | bytes 2631936 | tf_op jit(solution)/shard_map/cond/branch_1_fun/vhqk,vkhd->vhqd/dot_general | solution.py:29
  61.3 0.0 all-gather.3.cloned.1.call-done
  61.3 31.7 %all-gather.5.cloned.1.call-done = bf16[1,512,1280]{1,2,0:T(8,128)(2,1)} async-done(((bf16[1,128,1280]{1,2,0:T(8,128)(2,1)}), bf16[1,512,1280]{1,2,0:T(8,128)(2,1)}) %all-gather.5.cloned.1.call-update) | async-done | bytes 1310736 | tf_op jit(solution)/shard_map/all_gather | solution.py:69
  93.0 5.8 %conditional.3 = (f32[1,10,128]{2,1,0:T(8,128)S(1)}, f32[1,10,128,128]{2,3,1,0:T(8,128)S(1)}) conditional(s32[]{:T(128)} %convert_element_type.34, (f32[1,10,128]{2,1,0:T(8,128)S(1)}, f32[1,10,128,128]{3,2,1,0:T(8,128)}) %tuple.33, (pred[1,128,512]{2,1,0:T(8,128)(4,1)S(1)}, bf16[1,128,10,128]{1,3,2,0:T(8,128)(2,1)S(1)}, ...), branch_computations={%region_7.8_spmd, %region_8.11_spmd} | conditional | flops 344396800 | bytes 18946092 | solution.py:41
  93.1 2.0 %fusion.14 = (f32[10,128]{1,0:T(8,128)S(1)}, f32[10,128,512]{2,1,0:T(8,128)S(1)}) fusion(pred[128,512]{1,0:T(8,128)(4,1)S(1)} %bitcast.69, bf16[512,10,128]{0,2,1:T(8,128)(2,1)} %bitcast.67, bf16[1,128,10,128]{1,3,2,0:T(8,128)(2,1)S(1)} %get-tuple-element.188), kind=kOutput, calls=%fused_computation.22 | convolution fusion | flops 169736960 | bytes 4330496 | tf_op jit(solution)/shard_map/cond/branch_1_fun/vqhd,vkhd->vhqk/dot_general | solution.py:20
  95.1 0.0 copy-start.4
  95.1 0.9 fusion.16
  96.0 0.4 copy-done.4
  96.4 2.1 %fusion.27 = f32[1,10,128,128]{3,2,1,0:T(8,128)S(1)} fusion(bf16[512,10,128]{0,2,1:T(8,128)(2,1)S(1)} %bitcast.75, f32[10,128,512]{2,1,0:T(8,128)S(1)} %get-tuple-element.204, f32[10,128]{1,0:T(8,128)S(1)} %get-tuple-element.202, pred[128,512]{1,0:T(8,128)(4,1)S(1)} %bitcast.71, f32[1,10,128,128]{3,2,1,0:T(8,128)} %get-tuple-element.128, ...), kind=kOutput, calls=%fused_computation.32 | convolution fusion | flops 171376640 | bytes 5318656 | tf_op jit(solution)/shard_map/cond/branch_1_fun/vhqk,vkhd->vhqd/dot_general | solution.py:29
  98.6 0.2 copy.58
  98.8 0.1 divide_convert_fusion
  98.9 0.9 copy.53
  (14 shorter events, 0.2 us)
Async XLA Ops:
  6.5 7.1 %copy-start.2 = (bf16[1,2,32,1280]{3,2,1,0:T(8,128)(2,1)S(1)}, bf16[1,2,32,1280]{3,2,1,0:T(8,128)(2,1)}, u32[]{:S(2)}) copy-start(bf16[1,2,32,1280]{3,2,1,0:T(8,128)(2,1)} %param.16) | copy-start | bytes 491524
  6.5 29.8 %copy-start.3 = (s32[1,1,4]{2,1,0:T(1,128)S(1)}, s32[1,1,4]{2,1,0:T(1,128)}, u32[]{:S(2)}) copy-start(s32[1,1,4]{2,1,0:T(1,128)} %param.19) | copy-start | bytes 52
  6.5 33.2 %copy-start.5 = (s32[1,8]{1,0:T(1,128)S(1)}, s32[1,8]{1,0:T(1,128)}, u32[]{:S(2)}) copy-start(s32[1,8]{1,0:T(1,128)} %param.18) | copy-start | bytes 100
  6.5 33.3 %copy-start.6 = (s32[1,3]{1,0:T(1,128)S(1)}, s32[1,3]{1,0:T(1,128)}, u32[]{:S(2)}) copy-start(s32[1,3]{1,0:T(1,128)} %param.17) | copy-start | bytes 40
  6.5 47.0 %copy-start.1 = (bf16[1,128,1280]{2,1,0:T(8,128)(2,1)S(1)}, bf16[1,128,1280]{2,1,0:T(8,128)(2,1)}, u32[]{:S(2)}) copy-start(bf16[1,128,1280]{2,1,0:T(8,128)(2,1)} %param.12) | copy-start | bytes 983044
  6.5 54.8 %all-gather.3.cloned.1.call-start = ((), (), s32[]{:S(2)}) async-start(), calls=%async_computation | async-start | bytes 1638400 | tf_op jit(solution)/shard_map/all_gather | solution.py:68
  8.6 84.4 %all-gather.5.cloned.1.call-start = ((), (), s32[]{:S(2)}) async-start(), calls=%async_computation.1 | async-start | bytes 1638400 | tf_op jit(solution)/shard_map/all_gather | solution.py:69
  8.6 31.0 %collective-permute-start = (bf16[1,2,32,1280]{3,2,1,0:T(8,128)(2,1)}, bf16[1,2,32,1280]{3,2,1,0:T(8,128)(2,1)S(1)}, u32[]{:S(2)}, u32[]{:S(2)}) collective-permute-start(bf16[1,2,32,1280]{3,2,1,0:T(8,128)(2,1)} %param.15), channel_id=1, source_target_pairs={{0,4},{4,8},{8,12},{12,0},{1,5},{5,9},{9,13},{13,1},{2,6},{6,10},{... | collective-permute-start | bytes 491528 | tf_op jit(solution)/shard_map/ppermute | solution.py:57
  13.6 44.4 %copy-start = (bf16[1,2,32,1280]{3,2,1,0:T(8,128)(2,1)S(1)}, bf16[1,2,32,1280]{3,2,1,0:T(8,128)(2,1)}, u32[]{:S(2)}) copy-start(bf16[1,2,32,1280]{3,2,1,0:T(8,128)(2,1)} %param.15) | copy-start | bytes 491524
  39.7 10.8 %collective-permute-start.1 = (bf16[1,2,32,1280]{3,2,1,0:T(8,128)(2,1)S(1)}, bf16[1,2,32,1280]{3,2,1,0:T(8,128)(2,1)S(1)}, u32[]{:S(2)}, u32[]{:S(2)}) collective-permute-start(bf16[1,2,32,1280]{3,2,1,0:T(8,128)(2,1)S(1)} %collective-permute-done), channel_id=1, source_target_pairs={{0,4},{4,8},{8,12},{12,0},{1,5},{5,9},{9,13},{13,1},{2,6},{6,10},{... | collective-permute-start | bytes 491528 | tf_op jit(solution)/shard_map/ppermute | solution.py:57
  50.5 7.5 %collective-permute-start.2 = (bf16[1,2,32,1280]{3,2,1,0:T(8,128)(2,1)S(1)}, bf16[1,2,32,1280]{3,2,1,0:T(8,128)(2,1)S(1)}, u32[]{:S(2)}, u32[]{:S(2)}) collective-permute-start(bf16[1,2,32,1280]{3,2,1,0:T(8,128)(2,1)S(1)} %collective-permute-done.1), channel_id=1, source_target_pairs={{0,4},{4,8},{8,12},{12,0},{1,5},{5,9},{9,13},{13,1},{2,6},{6,10},{... | collective-permute-start | bytes 491528 | tf_op jit(solution)/shard_map/ppermute | solution.py:57
  95.1 1.3 %copy-start.4 = (bf16[1,512,1280]{1,2,0:T(8,128)(2,1)S(1)}, bf16[1,512,1280]{1,2,0:T(8,128)(2,1)}, u32[]{:S(2)}) copy-start(bf16[1,512,1280]{1,2,0:T(8,128)(2,1)} %get-tuple-element.129) | copy-start | bytes 3932164 | tf_op jit(solution)/shard_map/cond
Sparse Core Ops, SparseCore 0:
  8.9 47.7 all-gather.2
  58.3 34.6 all-gather.4
